TPU v7x, 32 devices: a whole 2x2x4 slice. The times are simulated.
32 devices in a mesh: seq: 16 (over z, y, x), wa: 2 (over core).
Axes of the slice: x: 2, y: 2, z: 4, core: 2. Of those that a mesh axis runs over, the one named last changes fastest.
Arguments:
- block_input: bfloat16 [16384, 1024], P('seq'), may hold values from -6 to 6
- doc_start: int32 [16384], P('seq'), may hold values from 0 to 16383, as said below
- norm1_gain: bfloat16 [1024], replicated, may hold values from 0.25 to 1.75
- in_weight: bfloat16 [3, 1024, 1024], P(None, 'seq', 'wa'), may hold values from -0.1875 to 0.1875
- conv_taps: bfloat16 [3, 1024], P(None, 'wa'), may hold values from -3 to 3
- out_weight: bfloat16 [1024, 1024], P('wa', 'seq'), may hold values from -0.1875 to 0.1875
- norm2_gain: bfloat16 [1024], replicated, may hold values from 0.25 to 1.75
- gate_weight: bfloat16 [1024, 4608], P('seq', 'wa'), may hold values from -0.1875 to 0.1875
- up_weight: bfloat16 [1024, 4608], P('seq', 'wa'), may hold values from -0.1875 to 0.1875
- down_weight: bfloat16 [4608, 1024], P('wa', 'seq'), may hold values from -0.09375 to 0.09375
- out_grad: bfloat16 [16384, 1024], P('seq'), may hold values from -6 to 6
Outputs:
- block_output: bfloat16 [16384, 1024], P('seq')
- input_grad: float32 [16384, 1024], P('seq')
- norm1_gain_grad: float32 [1024], replicated
- in_weight_grad: float32 [3, 1024, 1024], P(None, 'seq', 'wa')
- conv_taps_grad: float32 [3, 1024], P(None, 'wa')
- out_weight_grad: float32 [1024, 1024], P('wa', 'seq')
- norm2_gain_grad: float32 [1024], replicated
- gate_weight_grad: float32 [1024, 4608], P('seq', 'wa')
- up_weight_grad: float32 [1024, 4608], P('seq', 'wa')
- down_weight_grad: float32 [4608, 1024], P('wa', 'seq')
Inputs may be any that keep to these rules, and one draw needn't show every extreme that they name: doc_start[t] is the first token of the document that holds token t: documents are contiguous, doc_start never falls along the stream, doc_start[t] <= t, and doc_start[t] = t where a document begins; documents run across the borders of the seq shards; the first token and the last token of the stream each begin a document.
All inputs are finite; a program needn't handle non-finite values.
Results may differ from a plain program's by a relative error of at most 0.011.
Values may be sent and summed in bfloat16 or wider, within the bound.
No kernel may reach another device: no remote copies, remote signals or barrier semaphores. Data moves between devices by JAX's collectives and lax.ppermute only.
A program may use at most 192 MiB of HBM per device.

v0:
```python
import jax
import jax.numpy as jnp
from jax import lax
from jax.sharding import PartitionSpec as P

EPSILON = 1e-05


def shifted(value, axis, steps):
    count = lax.axis_size(axis)
    initial, last = (max(0, -steps), min(count, count - steps))
    return lax.ppermute(value, axis, [(source, source + steps) for source in range(initial, last)])


def tokens_product(first_op, second_op):
    return lax.dot_general(
        first_op, second_op, (((0,), (0,)), ((), ())), preferred_element_type=jnp.float32
    )


def back_product(first_op, second_op):
    return lax.dot_general(
        first_op, second_op, (((1,), (1,)), ((), ())), preferred_element_type=jnp.float32
    )


def local(
    block_input,
    doc_start,
    norm1_gain,
    in_weight,
    conv_taps,
    out_weight,
    norm2_gain,
    gate_weight,
    up_weight,
    down_weight,
    out_grad,
):
    row_count = block_input.shape[0]
    w_in, w_out, w_gate, w_up, w_down = (
        lax.all_gather(in_weight, "seq", axis=1, tiled=True),
        lax.all_gather(out_weight, "seq", axis=1, tiled=True),
        lax.all_gather(gate_weight, "seq", axis=0, tiled=True),
        lax.all_gather(up_weight, "seq", axis=0, tiled=True),
        lax.all_gather(down_weight, "seq", axis=1, tiled=True),
    )
    source = block_input.astype(jnp.float32)
    gain_one = norm1_gain.astype(jnp.float32)
    gain_two = norm2_gain.astype(jnp.float32)
    tap_vals = conv_taps.astype(jnp.float32)
    scale_one = lax.rsqrt(jnp.mean(source * source, axis=-1, keepdims=True) + EPSILON)
    hat_one = source * scale_one
    normed_in = (hat_one * gain_one).astype(jnp.bfloat16)
    projected = jnp.einsum("rd,jdc->jrc", normed_in, w_in, preferred_element_type=jnp.float32)
    proj_b = projected[0]
    proj_c = projected[1]
    proj_x = projected[2]
    mixed_rows = (proj_b * proj_x).astype(jnp.bfloat16)
    rim_rows = shifted(mixed_rows[row_count - 2 :], "seq", 1)
    extended = jnp.concatenate([rim_rows, mixed_rows], axis=0).astype(jnp.float32)
    mixed_now = extended[2:]
    back_one = extended[1 : row_count + 1]
    back_two = extended[:row_count]
    position = lax.axis_index("seq") * row_count + jnp.arange(row_count, dtype=jnp.int32)
    keep_one = (position - 1 >= doc_start)[:, None]
    keep_two = (position - 2 >= doc_start)[:, None]
    conv_out = (
        tap_vals[0] * mixed_now
        + jnp.where(keep_one, tap_vals[1] * back_one, 0.0)
        + jnp.where(keep_two, tap_vals[2] * back_two, 0.0)
    )
    gated_rows = (proj_c * conv_out).astype(jnp.bfloat16)
    mixer_out = lax.psum(jnp.dot(gated_rows, w_out, preferred_element_type=jnp.float32), "wa")
    residual = source + mixer_out
    scale_two = lax.rsqrt(jnp.mean(residual * residual, axis=-1, keepdims=True) + EPSILON)
    hat_two = residual * scale_two
    normed_mid = (hat_two * gain_two).astype(jnp.bfloat16)
    gate_pre = jnp.dot(normed_mid, w_gate, preferred_element_type=jnp.float32)
    up_pre = jnp.dot(normed_mid, w_up, preferred_element_type=jnp.float32)
    sigmoid_gate = jax.nn.sigmoid(gate_pre)
    hidden = (gate_pre * sigmoid_gate * up_pre).astype(jnp.bfloat16)
    ffn_out = lax.psum(
        jnp.dot(hidden, w_down, preferred_element_type=jnp.float32).astype(jnp.bfloat16), "wa"
    ).astype(jnp.float32)
    block_output = (residual + ffn_out).astype(jnp.bfloat16)
    down_grad = tokens_product(hidden, out_grad)
    d_hidden = back_product(out_grad, w_down)
    d_up = (d_hidden * gate_pre * sigmoid_gate).astype(jnp.bfloat16)
    d_gate = (d_hidden * up_pre * sigmoid_gate * (1.0 + gate_pre * (1.0 - sigmoid_gate))).astype(
        jnp.bfloat16
    )
    gate_grad = tokens_product(normed_mid, d_gate)
    up_grad = tokens_product(normed_mid, d_up)
    d_mid = lax.psum(back_product(d_gate, w_gate) + back_product(d_up, w_up), "wa")
    gain_two_grad = jnp.sum(d_mid * hat_two, axis=0)
    scaled_two = d_mid * gain_two
    d_resid = out_grad.astype(jnp.float32) + scale_two * (
        scaled_two - hat_two * jnp.mean(scaled_two * hat_two, axis=-1, keepdims=True)
    )
    d_mixer = d_resid.astype(jnp.bfloat16)
    mixer_grad = tokens_product(gated_rows, d_mixer)
    d_gated = back_product(d_mixer, w_out)
    d_conv = d_gated * proj_c
    d_proj_c = (d_gated * conv_out).astype(jnp.bfloat16)
    tap_grad = jnp.stack(
        [
            jnp.sum(d_conv * mixed_now, axis=0),
            jnp.sum(jnp.where(keep_one, d_conv * back_one, 0.0), axis=0),
            jnp.sum(jnp.where(keep_two, d_conv * back_two, 0.0), axis=0),
        ]
    )
    part_one = jnp.where(keep_one, tap_vals[1] * d_conv, 0.0)
    part_two = jnp.where(keep_two, tap_vals[2] * d_conv, 0.0)
    edge_rows = jnp.stack([part_two[0], part_one[0] + part_two[1]])
    incoming = shifted(edge_rows, "seq", -1)
    channels = d_conv.shape[1]
    d_mixed = (
        tap_vals[0] * d_conv
        + jnp.concatenate([part_one[1:], jnp.zeros((1, channels), jnp.float32)], axis=0)
        + jnp.concatenate([part_two[2:], jnp.zeros((2, channels), jnp.float32)], axis=0)
        + jnp.concatenate([jnp.zeros((row_count - 2, channels), jnp.float32), incoming], axis=0)
    )
    d_mixed_low = d_mixed.astype(jnp.bfloat16).astype(jnp.float32)
    d_proj = jnp.stack(
        [
            (d_mixed_low * proj_x).astype(jnp.bfloat16),
            d_proj_c,
            (d_mixed_low * proj_b).astype(jnp.bfloat16),
        ]
    )
    in_grad = jnp.einsum("rd,jrc->jdc", normed_in, d_proj, preferred_element_type=jnp.float32)
    d_norm_in = lax.psum(
        jnp.einsum("jrc,jdc->rd", d_proj, w_in, preferred_element_type=jnp.float32), "wa"
    )
    gain_one_grad = jnp.sum(d_norm_in * hat_one, axis=0)
    scaled_one = d_norm_in * gain_one
    input_grad = d_resid + scale_one * (
        scaled_one - hat_one * jnp.mean(scaled_one * hat_one, axis=-1, keepdims=True)
    )
    gain_one_total, gain_two_total, tap_total = lax.psum(
        (gain_one_grad, gain_two_grad, tap_grad), "seq"
    )
    in_share, mixer_share, gate_share, up_share, down_share = (
        lax.psum_scatter(in_grad, "seq", scatter_dimension=1, tiled=True),
        lax.psum_scatter(mixer_grad, "seq", scatter_dimension=1, tiled=True),
        lax.psum_scatter(gate_grad, "seq", scatter_dimension=0, tiled=True),
        lax.psum_scatter(up_grad, "seq", scatter_dimension=0, tiled=True),
        lax.psum_scatter(down_grad, "seq", scatter_dimension=1, tiled=True),
    )
    return (
        block_output,
        input_grad,
        gain_one_total,
        in_share,
        tap_total,
        mixer_share,
        gain_two_total,
        gate_share,
        up_share,
        down_share,
    )


def solution(mesh):
    placed = (
        P("seq", None),
        P("seq"),
        P(),
        P(None, "seq", "wa"),
        P(None, "wa"),
        P("wa", "seq"),
        P(),
        P("seq", "wa"),
        P("seq", "wa"),
        P("wa", "seq"),
        P("seq", None),
    )
    return jax.shard_map(
        local,
        mesh=mesh,
        in_specs=placed,
        out_specs=(
            P("seq", None),
            P("seq", None),
            P(),
            P(None, "seq", "wa"),
            P(None, "wa"),
            P("wa", "seq"),
            P(),
            P("seq", "wa"),
            P("seq", "wa"),
            P("wa", "seq"),
        ),
        check_vma=False,
    )
```

profile of v0, /device:TPU:0, one launch (start us, length us, event | category | flops | bytes accessed | tf_op | source)
XLA Modules:
  0.0 1446.9 jit_solution(15571177170516000621)
XLA Ops:
  12.3 68.8 %all-gather.6.cloned.1.call-done = bf16[3,1024,512]{2,1,0:T(8,128)(2,1)} async-done(((bf16[3,64,512]{2,1,0:T(8,128)(2,1)}), bf16[3,1024,512]{2,1,0:T(8,128)(2,1)}) %all-gather.6.cloned.1.call-update) | async-done | bytes 3145744 | tf_op jit(solution)/shard_map/all_gather | solution.py:42
  94.8 43.5 %all-gather.8.cloned.1.call-done = bf16[512,1024]{0,1:T(8,128)(2,1)} async-done(((bf16[512,64]{0,1:T(8,128)(2,1)}), bf16[512,1024]{0,1:T(8,128)(2,1)}) %all-gather.8.cloned.1.call-update) | async-done | bytes 1048592 | tf_op jit(solution)/shard_map/all_gather | solution.py:43
  144.8 25.4 %all-reduce.11.cloned.1.call-done = f32[1024,1024]{1,0:T(8,128)} async-done(((f32[1024,1024]{1,0:T(8,128)}), f32[1024,1024]{1,0:T(8,128)}) %all-reduce.11.cloned.1.call-update) | async-done | bytes 4194320 | tf_op jit(solution)/shard_map/psum | solution.py:74
  177.5 77.4 %all-gather.10.cloned.1.call-done = bf16[1024,2304]{1,0:T(8,128)(2,1)} async-done(((bf16[64,2304]{1,0:T(8,128)(2,1)}), bf16[1024,2304]{1,0:T(8,128)(2,1)}) %all-gather.10.cloned.1.call-update) | async-done | bytes 4718608 | tf_op jit(solution)/shard_map/all_gather | solution.py:44
  254.9 10.0 fusion.30
  264.9 72.1 %all-gather.12.cloned.1.call-done = bf16[1024,2304]{1,0:T(8,128)(2,1)} async-done(((bf16[64,2304]{1,0:T(8,128)(2,1)}), bf16[1024,2304]{1,0:T(8,128)(2,1)}) %all-gather.12.cloned.1.call-update) | async-done | bytes 4718608 | tf_op jit(solution)/shard_map/all_gather | solution.py:45
  337.1 10.1 fusion.31
  347.1 72.1 %all-gather.14.cloned.1.call-done = bf16[2304,1024]{0,1:T(8,128)(2,1)} async-done(((bf16[2304,64]{0,1:T(8,128)(2,1)}), bf16[2304,1024]{0,1:T(8,128)(2,1)}) %all-gather.14.cloned.1.call-update) | async-done | bytes 4718608 | tf_op jit(solution)/shard_map/all_gather | solution.py:46
  419.2 17.1 %multiply_convert_fusion = (bf16[1024,2304]{1,0:T(8,128)(2,1)S(1)}, bf16[1024,2304]{1,0:T(8,128)(2,1)}, bf16[1024,2304]{1,0:T(8,128)(2,1)}) fusion(f32[1024,2304]{1,0:T(8,128)} %fusion.30, f32[1024,2304]{1,0:T(8,128)} %fusion.31, bf16[1024,1024]{1,0:T(8,128)(2,1)} %param.21, bf16[2304,1024]{0,1:T(8,128)(2,1)} %all-gather.14.cloned.1.call-done), kind=kOutput, calls=%fused_computation | convolution fusion | flops 4869586944 | bytes 39845888 | tf_op jit(solution)/shard_map/dot_general | solution.py:22
  436.4 10.1 fusion.32
  453.4 9.3 convolution_convert_fusion
  462.8 17.5 %all-reduce.15.cloned.1.call-done = f32[1024,1024]{1,0:T(8,128)} async-done(((f32[1024,1024]{1,0:T(8,128)}), f32[1024,1024]{1,0:T(8,128)}) %all-reduce.15.cloned.1.call-update) | async-done | bytes 4194320 | tf_op jit(solution)/shard_map/psum | solution.py:95
  484.9 20.8 %all-reduce.13.cloned.1.call-done = bf16[1024,1024]{1,0:T(8,128)(2,1)} async-done(((bf16[1024,1024]{1,0:T(8,128)(2,1)}), bf16[1024,1024]{1,0:T(8,128)(2,1)}) %all-reduce.13.cloned.1.call-update) | async-done | bytes 2097168 | tf_op jit(solution)/shard_map/psum | solution.py:83
  535.3 8.5 convolution_bitcast_fusion
  543.8 9.7 copy.24
  558.8 10.6 fusion.33
  569.5 10.1 fusion.34
  580.0 10.1 fusion.35
  595.5 77.9 %all-reduce.4 = (f32[1024]{0:T(1024)}, f32[3,512]{1,0:T(4,128)}, f32[1024]{0:T(1024)}) all-reduce(f32[1024]{0:T(1024)S(1)} %get-tuple-element.32, f32[3,512]{1,0:T(4,128)S(1)} %pad_maximum_fusion.3, f32[1024]{0:T(1024)S(1)} %get-tuple-element.30), channel_id=1, replica_groups=mesh['seq'=16,'wa'=2] {'seq'}, use_global_device_ids=true, to_apply=%region_9.10 | all-reduce | flops 3584 | bytes 28672 | tf_op jit(solution)/shard_map/psum | solution.py:141
  678.9 149.9 %all-reduce.19.cloned.1.call-done = f32[3,1024,512]{2,0,1:T(4,128)} async-done(((f32[3,1024,512]{2,0,1:T(4,128)}), f32[3,1024,512]{2,0,1:T(4,128)}) %all-reduce.19.cloned.1.call-update) | async-done | bytes 6291472
  830.8 80.4 %reduce-scatter.5.cloned.1.call-done = f32[512,64]{0,1:T(8,128)} async-done(((f32[512,1024]{0,1:T(8,128)}), f32[512,64]{0,1:T(8,128)}) %reduce-scatter.5.cloned.1.call-update) | async-done | bytes 131088 | tf_op jit(solution)/shard_map/reduce_scatter | solution.py:146
  911.2 174.9 %reduce-scatter.7.cloned.1.call-done = f32[64,2304]{1,0:T(8,128)} async-done(((f32[1024,2304]{1,0:T(8,128)}), f32[64,2304]{1,0:T(8,128)}) %reduce-scatter.7.cloned.1.call-update) | async-done | bytes 589840 | tf_op jit(solution)/shard_map/reduce_scatter | solution.py:147
  1086.1 177.2 %reduce-scatter.9.cloned.1.call-done = f32[64,2304]{1,0:T(8,128)} async-done(((f32[1024,2304]{1,0:T(8,128)}), f32[64,2304]{1,0:T(8,128)}) %reduce-scatter.9.cloned.1.call-update) | async-done | bytes 589840 | tf_op jit(solution)/shard_map/reduce_scatter | solution.py:148
  1263.4 176.5 %reduce-scatter.11.cloned.1.call-done = f32[2304,64]{0,1:T(8,128)} async-done(((f32[2304,1024]{0,1:T(8,128)}), f32[2304,64]{0,1:T(8,128)}) %reduce-scatter.11.cloned.1.call-update) | async-done | bytes 589840 | tf_op jit(solution)/shard_map/reduce_scatter | solution.py:149
  (105 shorter events, 91.2 us)
Async XLA Ops:
  7.2 73.9 %all-gather.6.cloned.1.call-start = ((), (), s32[]{:S(2)}) async-start(), calls=%async_computation.4 | async-start | bytes 3342336 | tf_op jit(solution)/shard_map/all_gather | solution.py:42
  7.9 130.3 %all-gather.8.cloned.1.call-start = ((), (), s32[]{:S(2)}) async-start(), calls=%async_computation.5 | async-start | bytes 1114112 | tf_op jit(solution)/shard_map/all_gather | solution.py:43
  8.7 161.5 %all-reduce.11.cloned.1.call-start = ((), (), s32[]{:S(2)}) async-start(), calls=%async_computation.6 | async-start | bytes 8388608 | tf_op jit(solution)/shard_map/psum | solution.py:74
  87.1 5.4 copy-start.3
  87.1 3.8 copy-start.8
  87.5 4.7 collective-permute-start
  142.8 112.1 %all-gather.10.cloned.1.call-start = ((), (), s32[]{:S(2)}) async-start(), calls=%async_computation.7 | async-start | bytes 5013504 | tf_op jit(solution)/shard_map/all_gather | solution.py:44
  143.4 193.7 %all-gather.12.cloned.1.call-start = ((), (), s32[]{:S(2)}) async-start(), calls=%async_computation.8 | async-start | bytes 5013504 | tf_op jit(solution)/shard_map/all_gather | solution.py:45
  144.0 275.3 %all-gather.14.cloned.1.call-start = ((), (), s32[]{:S(2)}) async-start(), calls=%async_computation.9 | async-start | bytes 5013504 | tf_op jit(solution)/shard_map/all_gather | solution.py:46
  144.5 335.8 %all-reduce.15.cloned.1.call-start = ((), (), s32[]{:S(2)}) async-start(), calls=%async_computation.11 | async-start | bytes 8388608 | tf_op jit(solution)/shard_map/psum | solution.py:95
  436.4 10.1 copy-start.14
  436.4 10.1 copy-start.10
  453.2 52.5 %all-reduce.13.cloned.1.call-start = ((), (), s32[]{:S(2)}) async-start(), calls=%async_computation.10 | async-start | bytes 4194304 | tf_op jit(solution)/shard_map/psum | solution.py:83
  462.8 129.3 %all-reduce.17.cloned.1.call-start = ((), (), s32[]{:S(2)}) async-start(), calls=%async_computation.12 | async-start | bytes 8388608 | tf_op jit(solution)/shard_map/psum | solution.py:133
  505.7 6.7 copy-start.12
  518.2 8.2 copy-start.5
  518.2 6.6 slice-start
  519.0 5.8 slice-start.1
  519.0 5.8 collective-permute-start.1
  533.8 295.1 %all-reduce.19.cloned.1.call-start = ((), (), s32[]{:S(2)}) async-start(), calls=%async_computation.17 | async-start | bytes 16777216
  553.6 357.7 %reduce-scatter.5.cloned.1.call-start = ((), (), s32[]{:S(2)}) async-start(), calls=%async_computation.13 | async-start | bytes 2228224 | tf_op jit(solution)/shard_map/reduce_scatter | solution.py:146
  558.8 527.4 %reduce-scatter.7.cloned.1.call-start = ((), (), s32[]{:S(2)}) async-start(), calls=%async_computation.14 | async-start | bytes 10027008 | tf_op jit(solution)/shard_map/reduce_scatter | solution.py:147
  569.5 693.9 %reduce-scatter.9.cloned.1.call-start = ((), (), s32[]{:S(2)}) async-start(), calls=%async_computation.15 | async-start | bytes 10027008 | tf_op jit(solution)/shard_map/reduce_scatter | solution.py:148
  579.7 860.2 %reduce-scatter.11.cloned.1.call-start = ((), (), s32[]{:S(2)}) async-start(), calls=%async_computation.16 | async-start | bytes 10027008 | tf_op jit(solution)/shard_map/reduce_scatter | solution.py:149
  (9 other events, 16.2 us)
Sparse Core Ops, SparseCore 0:
  10.8 70.2 all-gather.5
  83.9 54.3 all-gather.7
  142.9 27.2 all-reduce.10
  173.2 81.6 all-gather.9
  257.9 79.0 all-gather.11
  340.1 79.0 all-gather.13
  453.3 27.0 all-reduce.14
  483.3 22.3 all-reduce.12
  533.9 30.4 all-reduce.16
  570.2 258.5 all-reduce.18
  831.7 79.5 reduce-scatter.4
  917.3 168.7 reduce-scatter.6
  1093.3 169.9 reduce-scatter.8
  1269.5 170.3 reduce-scatter.10
where the time goes:
time: 1450 us
  waiting for transfers between devices  1160 us (80%)
  matrix products  125 us (9%)
  blocking collectives  77.9 us (5%)
  other arithmetic  36.1 us (2%)
  local copies, waits for them, and re-layouts  21.7 us (1%)
  between operations  15.4 us (1%)
    reduce_scatter x1, waiting for transfers between devices, local(): lax.psum_scatter(up_grad, 'seq', scatter_dimension=0, tiled=True)  177 us
    reduce_scatter x1, waiting for transfers between devices, local(): lax.psum_scatter(down_grad, 'seq', scatter_dimension=1, tiled=True)  177 us
    reduce_scatter x1, waiting for transfers between devices, local(): lax.psum_scatter(gate_grad, 'seq', scatter_dimension=0, tiled=True)  175 us
    unnamed x15, waiting for transfers between devices  153 us
    reduce_scatter x1, waiting for transfers between devices, local(): lax.psum_scatter(mixer_grad, 'seq', scatter_dimension=1, tiled=True)  80.4 us
    psum x1, blocking collectives, local(): lax.psum((gain_one_grad, gain_two_grad, tap_grad), 'seq')  77.9 us
    all_gather x1, waiting for transfers between devices, local(): lax.all_gather(gate_weight, 'seq', axis=0, tiled=True)  77.4 us
    all_gather x1, waiting for transfers between devices, local(): lax.all_gather(up_weight, 'seq', axis=0, tiled=True)  72.1 us
  transfers between devices with their start and end apart: 16, of which 15 were waited for; matrix products, arithmetic and copies ran while one was open for 8% of the time, Pallas kernels for 0%

commit v1 on v0

v1 whole, which is shorter than its diff:
```python
import jax
import jax.numpy as jnp
from jax import lax
from jax.experimental import pallas as pl
from jax.experimental.pallas import tpu as pltpu
from jax.sharding import PartitionSpec as P

EPSILON = 1e-05
F32 = jnp.float32
BF16 = jnp.bfloat16


def shifted(value, axis, steps):
    count = lax.axis_size(axis)
    initial, last = (max(0, -steps), min(count, count - steps))
    return lax.ppermute(value, axis, [(source, source + steps) for source in range(initial, last)])


def partner(value, bits):
    return lax.ppermute(value, "seq", [(i, i ^ bits) for i in range(lax.axis_size("seq"))])


def both_cores(value):
    low = value.astype(BF16)
    return low.astype(F32) + lax.ppermute(low, "wa", [(0, 1), (1, 0)]).astype(F32)


def on_block():
    return lax.axis_size("seq") == 16 and lax.axis_size("wa") == 2


def place_kernel(own, side, ahead, corner_a, corner_b, full, buf, sems, out_sem):
    index = lax.axis_index("seq")
    z, y, x = index // 4, (index // 2) % 2, index % 2
    copies = []
    for k in range(4):
        plane = (z ^ k) * 4
        corner = corner_a if k < 2 else corner_b
        for source, row, yy, xx in (
            (own, k, y, x),
            (side, k, y, 1 - x),
            (ahead, k, 1 - y, x),
            (corner, k % 2, 1 - y, 1 - x),
        ):
            copy = pltpu.make_async_copy(
                source.at[row], buf.at[plane + yy * 2 + xx], sems.at[len(copies)]
            )
            copy.start()
            copies.append(copy)
    for copy in copies:
        copy.wait()
    last = pltpu.make_async_copy(buf, full, out_sem)
    last.start()
    last.wait()


def gather_rows(shard):
    rows, columns = shard.shape
    if not on_block():
        return lax.all_gather(shard, "seq", axis=0, tiled=True)
    own = jnp.stack([shard, partner(shard, 4), partner(shard, 8), partner(shard, 12)])
    side, ahead = partner(own, 1), partner(own, 2)
    corner_a, corner_b = partner(ahead[:2], 1), partner(side[2:], 2)
    full = pl.pallas_call(
        place_kernel,
        out_shape=jax.ShapeDtypeStruct((16, rows, columns), shard.dtype),
        in_specs=[pl.BlockSpec(memory_space=pl.ANY)] * 5,
        out_specs=pl.BlockSpec(memory_space=pl.ANY),
        scratch_shapes=[
            pltpu.VMEM((16, rows, columns), shard.dtype),
            pltpu.SemaphoreType.DMA((16,)),
            pltpu.SemaphoreType.DMA,
        ],
        compiler_params=pltpu.CompilerParams(vmem_limit_bytes=24 * 2**20),
        cost_estimate=pl.CostEstimate(flops=0, bytes_accessed=64 * rows * columns, transcendentals=0),
    )(own, side, ahead, corner_a, corner_b)
    return full.reshape(16 * rows, columns)


def scatter_rows(partial):
    if not on_block():
        return lax.psum_scatter(partial.astype(F32), "seq", scatter_dimension=0, tiled=True)
    rows, columns = partial.shape[0] // 16, partial.shape[1]
    blocks = partial.astype(BF16).reshape(4, 2, 2, rows, columns)
    index = lax.axis_index("seq")
    z, y, x = index // 4, (index // 2) % 2, index % 2

    def quarter(yy, xx):
        return lax.dynamic_slice(blocks, (0, yy, xx, 0, 0), (4, 1, 1, rows, columns)).reshape(
            4, rows, columns
        )

    corner = quarter(1 - y, 1 - x)
    from_side, from_ahead = partner(corner[:2], 1), partner(corner[2:], 2)
    ahead, side = quarter(1 - y, x), quarter(y, 1 - x)
    ahead = jnp.concatenate([(ahead[:2].astype(F32) + from_side.astype(F32)).astype(BF16), ahead[2:]])
    side = jnp.concatenate([side[:2], (side[2:].astype(F32) + from_ahead.astype(F32)).astype(BF16)])
    got_ahead, got_side = partner(ahead, 2), partner(side, 1)
    column = quarter(y, x).astype(F32) + got_ahead.astype(F32) + got_side.astype(F32)
    total = lax.dynamic_index_in_dim(column, z, 0, keepdims=False)
    for k in (1, 2, 3):
        part = lax.dynamic_index_in_dim(column, z ^ k, 0, keepdims=False).astype(BF16)
        total = total + partner(part, 4 * k).astype(F32)
    return total


def sum_all(value):
    if not on_block():
        return lax.psum(value, "seq")
    for bits in (1, 2, 4, 8):
        value = value + partner(value, bits)
    return value


def tokens_product(first_op, second_op):
    return lax.dot_general(
        first_op, second_op, (((0,), (0,)), ((), ())), preferred_element_type=F32
    )


def back_product(first_op, second_op):
    return lax.dot_general(
        first_op, second_op, (((1,), (1,)), ((), ())), preferred_element_type=F32
    )


def product(first_op, second_op):
    return jnp.dot(first_op, second_op, preferred_element_type=F32)


def local(
    block_input,
    doc_start,
    norm1_gain,
    in_weight,
    conv_taps,
    out_weight,
    norm2_gain,
    gate_weight,
    up_weight,
    down_weight,
    out_grad,
):
    row_count = block_input.shape[0]
    shard_rows, channels = in_weight.shape[1:]
    mixer_shard = jnp.concatenate(
        [in_weight[0], in_weight[1], in_weight[2], out_weight.T], axis=1
    )
    w_mixer = gather_rows(mixer_shard)
    w_gate = gather_rows(gate_weight)
    w_up = gather_rows(up_weight)
    w_down = gather_rows(down_weight.T)
    w_in, w_out = w_mixer[:, : 3 * channels], w_mixer[:, 3 * channels :]
    source = block_input.astype(F32)
    gain_one = norm1_gain.astype(F32)
    gain_two = norm2_gain.astype(F32)
    tap_vals = conv_taps.astype(F32)
    scale_one = lax.rsqrt(jnp.mean(source * source, axis=-1, keepdims=True) + EPSILON)
    hat_one = source * scale_one
    normed_in = (hat_one * gain_one).astype(BF16)
    projected = product(normed_in, w_in)
    proj_b = projected[:, :channels]
    proj_c = projected[:, channels : 2 * channels]
    proj_x = projected[:, 2 * channels :]
    mixed_rows = (proj_b * proj_x).astype(BF16)
    rim_rows = shifted(mixed_rows[row_count - 2 :], "seq", 1)
    extended = jnp.concatenate([rim_rows, mixed_rows], axis=0).astype(F32)
    mixed_now = extended[2:]
    back_one = extended[1 : row_count + 1]
    back_two = extended[:row_count]
    position = lax.axis_index("seq") * row_count + jnp.arange(row_count, dtype=jnp.int32)
    keep_one = (position - 1 >= doc_start)[:, None]
    keep_two = (position - 2 >= doc_start)[:, None]
    conv_out = (
        tap_vals[0] * mixed_now
        + jnp.where(keep_one, tap_vals[1] * back_one, 0.0)
        + jnp.where(keep_two, tap_vals[2] * back_two, 0.0)
    )
    gated_rows = (proj_c * conv_out).astype(BF16)
    mixer_out = both_cores(back_product(gated_rows, w_out))
    residual = source + mixer_out
    scale_two = lax.rsqrt(jnp.mean(residual * residual, axis=-1, keepdims=True) + EPSILON)
    hat_two = residual * scale_two
    normed_mid = (hat_two * gain_two).astype(BF16)
    gate_pre = product(normed_mid, w_gate)
    up_pre = product(normed_mid, w_up)
    sigmoid_gate = jax.nn.sigmoid(gate_pre)
    hidden = (gate_pre * sigmoid_gate * up_pre).astype(BF16)
    down_share = scatter_rows(tokens_product(out_grad, hidden))
    ffn_out = both_cores(back_product(hidden, w_down))
    block_output = (residual + ffn_out).astype(BF16)
    d_hidden = product(out_grad, w_down)
    d_up = (d_hidden * gate_pre * sigmoid_gate).astype(BF16)
    d_gate = (d_hidden * up_pre * sigmoid_gate * (1.0 + gate_pre * (1.0 - sigmoid_gate))).astype(
        BF16
    )
    gate_share = scatter_rows(tokens_product(normed_mid, d_gate))
    up_share = scatter_rows(tokens_product(normed_mid, d_up))
    d_mid = both_cores(back_product(d_gate, w_gate) + back_product(d_up, w_up))
    gain_two_grad = jnp.sum(d_mid * hat_two, axis=0)
    scaled_two = d_mid * gain_two
    d_resid = out_grad.astype(F32) + scale_two * (
        scaled_two - hat_two * jnp.mean(scaled_two * hat_two, axis=-1, keepdims=True)
    )
    d_mixer = d_resid.astype(BF16)
    mixer_grad = tokens_product(d_mixer, gated_rows)
    d_gated = product(d_mixer, w_out)
    d_conv = d_gated * proj_c
    d_proj_c = (d_gated * conv_out).astype(BF16)
    tap_grad = jnp.stack(
        [
            jnp.sum(d_conv * mixed_now, axis=0),
            jnp.sum(jnp.where(keep_one, d_conv * back_one, 0.0), axis=0),
            jnp.sum(jnp.where(keep_two, d_conv * back_two, 0.0), axis=0),
        ]
    )
    part_one = jnp.where(keep_one, tap_vals[1] * d_conv, 0.0)
    part_two = jnp.where(keep_two, tap_vals[2] * d_conv, 0.0)
    edge_rows = jnp.stack([part_two[0], part_one[0] + part_two[1]])
    incoming = shifted(edge_rows, "seq", -1)
    d_mixed = (
        tap_vals[0] * d_conv
        + jnp.concatenate([part_one[1:], jnp.zeros((1, channels), F32)], axis=0)
        + jnp.concatenate([part_two[2:], jnp.zeros((2, channels), F32)], axis=0)
        + jnp.concatenate([jnp.zeros((row_count - 2, channels), F32), incoming], axis=0)
    )
    d_mixed_low = d_mixed.astype(BF16).astype(F32)
    d_proj = jnp.concatenate(
        [
            (d_mixed_low * proj_x).astype(BF16),
            d_proj_c,
            (d_mixed_low * proj_b).astype(BF16),
        ],
        axis=1,
    )
    in_grad = tokens_product(normed_in, d_proj)
    mixer_share = scatter_rows(jnp.concatenate([in_grad, mixer_grad], axis=1))
    d_norm_in = both_cores(back_product(d_proj, w_in))
    gain_one_grad = jnp.sum(d_norm_in * hat_one, axis=0)
    scaled_one = d_norm_in * gain_one
    input_grad = d_resid + scale_one * (
        scaled_one - hat_one * jnp.mean(scaled_one * hat_one, axis=-1, keepdims=True)
    )
    width = gain_one.shape[0]
    small = jnp.concatenate(
        [gain_one_grad[None], gain_two_grad[None], jnp.pad(tap_grad, ((0, 0), (0, width - channels)))]
    )
    small = sum_all(small)
    in_share = mixer_share[:, : 3 * channels].reshape(shard_rows, 3, channels).transpose(1, 0, 2)
    return (
        block_output,
        input_grad,
        small[0],
        in_share,
        small[2:, :channels],
        mixer_share[:, 3 * channels :].T,
        small[1],
        gate_share,
        up_share,
        down_share.T,
    )


def solution(mesh):
    placed = (
        P("seq", None),
        P("seq"),
        P(),
        P(None, "seq", "wa"),
        P(None, "wa"),
        P("wa", "seq"),
        P(),
        P("seq", "wa"),
        P("seq", "wa"),
        P("wa", "seq"),
        P("seq", None),
    )
    return jax.shard_map(
        local,
        mesh=mesh,
        in_specs=placed,
        out_specs=(
            P("seq", None),
            P("seq", None),
            P(),
            P(None, "seq", "wa"),
            P(None, "wa"),
            P("wa", "seq"),
            P(),
            P("seq", "wa"),
            P("seq", "wa"),
            P("wa", "seq"),
        ),
        check_vma=False,
    )
```

time: 1450 us -> 557 us (0.38)
  waiting for transfers between devices: 1160 us -> 222 us
  starting transfers between devices: 6.4 us -> 142 us
  blocking collectives: 77.9 us -> 0 us
  matrix products: 125 us -> 92.6 us
  local copies, waits for them, and re-layouts: 21.7 us -> 38.4 us
    reduce_scatter x4 -> x0, waiting for transfers between devices: 609 us -> none  [the longest x1 177 us: local(): lax.psum_scatter(up_grad, 'seq', scatter_dimension=0, tiled=True)]
    all_gather x5 -> x0, waiting for transfers between devices: 334 us -> none  [the longest x1 77.4 us: local(): lax.all_gather(gate_weight, 'seq', axis=0, tiled=True)]
    ppermute x0 -> x64, waiting for transfers between devices: none -> 207 us  [the longest x60 207 us: partner(): lax.ppermute(value, 'seq', [(i, i ^ bits) for i in range(lax.axis_size('s...]
    unnamed x15 -> x0, waiting for transfers between devices: 153 us -> none
    ppermute x0 -> x64, starting transfers between devices: none -> 137 us  [the longest x60 137 us: partner(): lax.ppermute(value, 'seq', [(i, i ^ bits) for i in range(lax.axis_size('s...]
    psum x1 -> x0, blocking collectives: 77.9 us -> none  [local(): lax.psum((gain_one_grad, gain_two_grad, tap_grad), 'seq')]
    psum x4 -> x0, waiting for transfers between devices: 63.8 us -> none  [the longest x1 25.4 us: local(): lax.psum(jnp.dot(gated_rows, w_out, preferred_element_type=jnp.float32),...]
    unnamed x37 -> x147, local copies, waits for them, and re-layouts: 10.7 us -> 28.3 us
  transfers between devices with their start and end apart: 16 -> 66, of which waited for: 15 -> 28; matrix products, arithmetic and copies ran while one was open for 8% -> 19% of each run, Pallas kernels for 0% -> 1%
where the time goes in v1:
time: 557 us; the launch traced here: 550 us
  waiting for transfers between devices  222 us (40%)
  starting transfers between devices  142 us (25%)
  matrix products  92.6 us (17%)
  other arithmetic  45.5 us (8%)
  local copies, waits for them, and re-layouts  38.4 us (7%)
  Pallas kernels  6.82 us (1%)
    ppermute x60, waiting for transfers between devices, partner(): lax.ppermute(value, 'seq', [(i, i ^ bits) for i in range(lax.axis_size('s...  207 us
    ppermute x60, starting transfers between devices, partner(): lax.ppermute(value, 'seq', [(i, i ^ bits) for i in range(lax.axis_size('s...  137 us
    dot_general x5, matrix products, product(): return jnp.dot(first_op, second_op, preferred_element_type=F32)  40.3 us
    unnamed x147, local copies, waits for them, and re-layouts  28.3 us
    dot_general x5, matrix products, back_product(): lax.dot_general(first_op, second_op, (((1,), (1,)), ((), ())), preferred_...  26.5 us
    dot_general x5, matrix products, tokens_product(): lax.dot_general(first_op, second_op, (((0,), (0,)), ((), ())), preferred_...  25.8 us
    ppermute x2, waiting for transfers between devices, shifted(): lax.ppermute(value, axis, [(source, source + steps) for source in range(i...  15.8 us
  transfers between devices with their start and end apart: 66, of which 28 were waited for; matrix products, arithmetic and copies ran while one was open for 19% of the time, Pallas kernels for 1%

profile of v1, /device:TPU:0, one launch (start us, length us, event | category | flops | bytes accessed | tf_op | source)
XLA Modules:
  0.0 550.1 jit_solution(11335277683149219700)
XLA Ops:
  8.1 8.6 %collective-permute-done = bf16[64,2048]{1,0:T(8,128)(2,1)S(1)} collective-permute-done((bf16[64,2048]{1,0:T(8,128)(2,1)S(1)}, bf16[64,2048]{1,0:T(8,128)(2,1)S(1)}, u32[]{:S(2)}, u32[]{:S(2)}) %collective-permute-start) | collective-permute-done | bytes 262176 | tf_op jit(solution)/shard_map/ppermute | solution.py:20
  16.7 10.2 %collective-permute-done.1 = bf16[64,2048]{1,0:T(8,128)(2,1)S(1)} collective-permute-done((bf16[64,2048]{1,0:T(8,128)(2,1)S(1)}, bf16[64,2048]{1,0:T(8,128)(2,1)S(1)}, u32[]{:S(2)}, u32[]{:S(2)}) %collective-permute-start.1) | collective-permute-done | bytes 262176 | tf_op jit(solution)/shard_map/ppermute | solution.py:20
  65.2 13.3 %collective-permute-start.16 = (bf16[64,2304]{1,0:T(8,128)(2,1)S(1)}, bf16[64,2304]{1,0:T(8,128)(2,1)S(1)}, u32[]{:S(2)}, u32[]{:S(2)}) collective-permute-start(bf16[64,2304]{1,0:T(8,128)(2,1)S(1)} %copy-done.44), channel_id=1, source_target_pairs={{0,8},{2,10},{4,12},{6,14},{8,0},{10,2},{12,4},{14,6},{16,24},{18,... | collective-permute-start | bytes 884744 | tf_op jit(solution)/shard_map/ppermute | solution.py:20
  78.5 8.7 %collective-permute-done.24 = bf16[64,2304]{1,0:T(8,128)(2,1)S(1)} collective-permute-done((bf16[64,2304]{1,0:T(8,128)(2,1)}, bf16[64,2304]{1,0:T(8,128)(2,1)S(1)}, u32[]{:S(2)}, u32[]{:S(2)}) %collective-permute-start.24) | collective-permute-done | bytes 294944 | tf_op jit(solution)/shard_map/ppermute | solution.py:20
  99.9 9.3 %collective-permute-done.17 = bf16[64,2304]{1,0:T(8,128)(2,1)S(1)} collective-permute-done((bf16[64,2304]{1,0:T(8,128)(2,1)S(1)}, bf16[64,2304]{1,0:T(8,128)(2,1)S(1)}, u32[]{:S(2)}, u32[]{:S(2)}) %collective-permute-start.17) | collective-permute-done | bytes 294944 | tf_op jit(solution)/shard_map/ppermute | solution.py:20
  113.4 7.9 %collective-permute-done.13.ahead = bf16[4,64,2304]{2,1,0:T(8,128)(2,1)S(1)} collective-permute-done((bf16[4,64,2304]{2,1,0:T(8,128)(2,1)S(1)}, bf16[4,64,2304]{2,1,0:T(8,128)(2,1)S(1)}, u32[]{:S(2)}, u32[]{:S(2)}) %collective-permute-start.13) | collective-permute-done | bytes 1179680 | tf_op jit(solution)/shard_map/ppermute | solution.py:20
  122.5 13.6 %collective-permute-done.7 = bf16[2,512]{1,0:T(2,128)(2,1)S(1)} collective-permute-done((bf16[2,512]{1,0:T(2,128)(2,1)S(1)}, bf16[2,512]{1,0:T(2,128)(2,1)S(1)}, u32[]{:S(2)}, u32[]{:S(2)}) %collective-permute-start.7) | collective-permute-done | bytes 2080 | tf_op jit(solution)/shard_map/ppermute | solution.py:16
  151.6 20.0 %collective-permute-done.20.ahead = bf16[4,64,2304]{2,1,0:T(8,128)(2,1)S(1)} collective-permute-done((bf16[4,64,2304]{2,1,0:T(8,128)(2,1)S(1)}, bf16[4,64,2304]{2,1,0:T(8,128)(2,1)S(1)}, u32[]{:S(2)}, u32[]{:S(2)}) %collective-permute-start.20) | collective-permute-done | bytes 1179680 | tf_op jit(solution)/shard_map/ppermute | solution.py:20
  213.3 7.6 %fusion.79 = f32[1024,2304]{1,0:T(8,128)} fusion(bf16[1024,1024]{0,1:T(8,128)(2,1)S(1)} %multiply_convert_fusion.1, bf16[1024,2304]{1,0:T(8,128)(2,1)S(1)} %bitcast.289), kind=kOutput, calls=%fused_computation.203 | convolution fusion | flops 4831838208 | bytes 16252928 | tf_op jit(solution)/shard_map/dot_general | solution.py:128
  221.0 19.5 %fusion.2 = (bf16[1024,2304]{1,0:T(8,128)(2,1)}, bf16[1024,2304]{1,0:T(8,128)(2,1)}, bf16[1024,2304]{1,0:T(8,128)(2,1)}) fusion(f32[2304,1024]{0,1:T(8,128)} %fusion.81, f32[1024,2304]{1,0:T(8,128)} %fusion.79, bf16[1024,1024]{0,1:T(8,128)(2,1)} %copy-done.39, bf16[1024,2304]{1,0:T(8,128)(2,1)} %bitcast.295), kind=kOutput, calls=%fused_computation.4 | convolution fusion | flops 4869586944 | bytes 39845888 | tf_op jit(solution)/shard_map/dot_general | solution.py:128
  240.5 8.2 %convolution_convert_fusion = bf16[2304,1024]{0,1:T(8,128)(2,1)S(1)} fusion(bf16[1024,2304]{1,0:T(8,128)(2,1)} %get-tuple-element.46, bf16[1024,1024]{1,0:T(8,128)(2,1)} %param.21), kind=kOutput, calls=%fused_computation.20 | convolution fusion | flops 4834197504 | bytes 11534336 | tf_op jit(solution)/shard_map/dot_general | solution.py:116
  270.1 7.6 %convolution_convert_fusion.2 = bf16[1024,2304]{1,0:T(8,128)(2,1)S(1)} fusion(bf16[1024,1024]{0,1:T(8,128)(2,1)S(1)} %copy-done.40, bf16[1024,2304]{1,0:T(8,128)(2,1)} %get-tuple-element.44), kind=kOutput, calls=%fused_computation.22 | convolution fusion | flops 4834197504 | bytes 11534336 | tf_op jit(solution)/shard_map/dot_general | solution.py:116
  278.4 7.8 %add_convert_fusion = bf16[1024,1024]{0,1:T(8,128)(2,1)S(1)} fusion(f32[1024,1024]{0,1:T(8,128)S(1)} %fusion.80, bf16[1024,2304]{1,0:T(8,128)(2,1)} %get-tuple-element.44, bf16[1024,2304]{1,0:T(8,128)(2,1)S(1)} %bitcast.290), kind=kOutput, calls=%fused_computation.39 | convolution fusion | flops 4833935360 | bytes 15728640 | tf_op jit(solution)/shard_map/dot_general | solution.py:122
  297.3 10.1 %collective-permute-done.45 = bf16[2,64,2304]{2,1,0:T(8,128)(2,1)S(1)} collective-permute-done((bf16[2,64,2304]{2,1,0:T(8,128)(2,1)S(1)}, bf16[2,64,2304]{2,1,0:T(8,128)(2,1)S(1)}, u32[]{:S(2)}, u32[]{:S(2)}) %collective-permute-start.45) | collective-permute-done | bytes 589856 | tf_op jit(solution)/shard_map/ppermute | solution.py:20
  309.9 23.2 %collective-permute-done.60 = bf16[4,64,2304]{2,1,0:T(8,128)(2,1)S(1)} collective-permute-done((bf16[4,64,2304]{2,1,0:T(8,128)(2,1)S(1)}, bf16[4,64,2304]{2,1,0:T(8,128)(2,1)S(1)}, u32[]{:S(2)}, u32[]{:S(2)}) %collective-permute-start.60) | collective-permute-done | bytes 1179680 | tf_op jit(solution)/shard_map/ppermute | solution.py:20
  337.0 21.4 %collective-permute-done.53 = bf16[4,64,2304]{2,1,0:T(8,128)(2,1)S(1)} collective-permute-done((bf16[4,64,2304]{2,1,0:T(8,128)(2,1)S(1)}, bf16[4,64,2304]{2,1,0:T(8,128)(2,1)S(1)}, u32[]{:S(2)}, u32[]{:S(2)}) %collective-permute-start.53) | collective-permute-done | bytes 1179680 | tf_op jit(solution)/shard_map/ppermute | solution.py:20
  358.4 12.4 %collective-permute-start.63 = (bf16[64,2304]{1,0:T(8,128)(2,1)S(1)}, bf16[64,2304]{1,0:T(8,128)(2,1)S(1)}, u32[]{:S(2)}, u32[]{:S(2)}) collective-permute-start(bf16[64,2304]{1,0:T(8,128)(2,1)S(1)} %get-tuple-element.70), channel_id=1, source_target_pairs={{0,8},{2,10},{4,12},{6,14},{8,0},{10,2},{12,4},{14,6},{16,24},{18,... | collective-permute-start | bytes 884744 | tf_op jit(solution)/shard_map/ppermute | solution.py:20
  371.2 7.6 %collective-permute-done.46 = bf16[4,64,2304]{2,1,0:T(8,128)(2,1)S(1)} collective-permute-done((bf16[4,64,2304]{2,1,0:T(8,128)(2,1)S(1)}, bf16[4,64,2304]{2,1,0:T(8,128)(2,1)S(1)}, u32[]{:S(2)}, u32[]{:S(2)}) %collective-permute-start.46) | collective-permute-done | bytes 1179680 | tf_op jit(solution)/shard_map/ppermute | solution.py:20
  378.8 11.9 %collective-permute-start.64 = (bf16[64,2304]{1,0:T(8,128)(2,1)S(1)}, bf16[64,2304]{1,0:T(8,128)(2,1)S(1)}, u32[]{:S(2)}, u32[]{:S(2)}) collective-permute-start(bf16[64,2304]{1,0:T(8,128)(2,1)S(1)} %get-tuple-element.72), channel_id=1, source_target_pairs={{0,16},{2,18},{4,20},{6,22},{8,24},{10,26},{12,28},{14,30},{16,0},... | collective-permute-start | bytes 884744 | tf_op jit(solution)/shard_map/ppermute | solution.py:20
  395.1 18.2 %collective-permute-done.64 = bf16[64,2304]{1,0:T(8,128)(2,1)S(1)} collective-permute-done((bf16[64,2304]{1,0:T(8,128)(2,1)S(1)}, bf16[64,2304]{1,0:T(8,128)(2,1)S(1)}, u32[]{:S(2)}, u32[]{:S(2)}) %collective-permute-start.64) | collective-permute-done | bytes 294944 | tf_op jit(solution)/shard_map/ppermute | solution.py:20
  445.3 12.3 %collective-permute-start.40 = (bf16[2,64,2048]{2,1,0:T(8,128)(2,1)S(1)}, bf16[2,64,2048]{2,1,0:T(8,128)(2,1)S(1)}, u32[]{:S(2)}, u32[]{:S(2)}) collective-permute-start(bf16[2,64,2048]{2,1,0:T(8,128)(2,1)S(1)} %get-tuple-element.88), channel_id=1, source_target_pairs={{0,4},{2,6},{4,0},{6,2},{8,12},{10,14},{12,8},{14,10},{16,20},{18,... | collective-permute-start | bytes 1572872 | tf_op jit(solution)/shard_map/ppermute | solution.py:20
  457.7 8.3 %collective-permute-start.49 = (bf16[64,2304]{1,0:T(8,128)(2,1)S(1)}, bf16[64,2304]{1,0:T(8,128)(2,1)S(1)}, u32[]{:S(2)}, u32[]{:S(2)}) collective-permute-start(bf16[64,2304]{1,0:T(8,128)(2,1)S(1)} %copy-done.47), channel_id=1, source_target_pairs={{0,8},{2,10},{4,12},{6,14},{8,0},{10,2},{12,4},{14,6},{16,24},{18,... | collective-permute-start | bytes 884744 | tf_op jit(solution)/shard_map/ppermute | solution.py:20
  490.5 8.1 %collective-permute-done.39 = bf16[4,64,2048]{2,1,0:T(8,128)(2,1)} collective-permute-done((bf16[4,64,2048]{2,1,0:T(8,128)(2,1)}, bf16[4,64,2048]{2,1,0:T(8,128)(2,1)}, u32[]{:S(2)}, u32[]{:S(2)}) %collective-permute-start.39) | collective-permute-done | bytes 1048608 | tf_op jit(solution)/shard_map/ppermute | solution.py:20
  513.5 10.4 %collective-permute-done.43 = bf16[64,2048]{1,0:T(8,128)(2,1)S(1)} collective-permute-done((bf16[64,2048]{1,0:T(8,128)(2,1)S(1)}, bf16[64,2048]{1,0:T(8,128)(2,1)S(1)}, u32[]{:S(2)}, u32[]{:S(2)}) %collective-permute-start.43) | collective-permute-done | bytes 262176 | tf_op jit(solution)/shard_map/ppermute | solution.py:20
  (361 shorter events, 261.4 us)
Async XLA Ops:
  59.4 33.0 %collective-permute-start.5 = (bf16[2,64,2048]{2,1,0:T(8,128)(2,1)S(1)}, bf16[2,64,2048]{2,1,0:T(8,128)(2,1)S(1)}, u32[]{:S(2)}, u32[]{:S(2)}) collective-permute-start(bf16[2,64,2048]{2,1,0:T(8,128)(2,1)S(1)} %slice.303), channel_id=1, source_target_pairs={{0,2},{2,0},{4,6},{6,4},{8,10},{10,8},{12,14},{14,12},{16,18},{18,... | collective-permute-start | bytes 1572872 | tf_op jit(solution)/shard_map/ppermute | solution.py:20
  60.8 32.1 %collective-permute-start.6 = (bf16[2,64,2048]{2,1,0:T(8,128)(2,1)S(1)}, bf16[2,64,2048]{2,1,0:T(8,128)(2,1)S(1)}, u32[]{:S(2)}, u32[]{:S(2)}) collective-permute-start(bf16[2,64,2048]{2,1,0:T(8,128)(2,1)S(1)} %slice.304), channel_id=1, source_target_pairs={{0,4},{2,6},{4,0},{6,2},{8,12},{10,14},{12,8},{14,10},{16,20},{18,... | collective-permute-start | bytes 1572872 | tf_op jit(solution)/shard_map/ppermute | solution.py:20
  65.2 32.7 %collective-permute-start.16 = (bf16[64,2304]{1,0:T(8,128)(2,1)S(1)}, bf16[64,2304]{1,0:T(8,128)(2,1)S(1)}, u32[]{:S(2)}, u32[]{:S(2)}) collective-permute-start(bf16[64,2304]{1,0:T(8,128)(2,1)S(1)} %copy-done.44), channel_id=1, source_target_pairs={{0,8},{2,10},{4,12},{6,14},{8,0},{10,2},{12,4},{14,6},{16,24},{18,... | collective-permute-start | bytes 884744 | tf_op jit(solution)/shard_map/ppermute | solution.py:20
  97.9 48.7 %collective-permute-start.27 = (bf16[4,64,2304]{2,1,0:T(8,128)(2,1)S(1)}, bf16[4,64,2304]{2,1,0:T(8,128)(2,1)S(1)}, u32[]{:S(2)}, u32[]{:S(2)}) collective-permute-start(bf16[4,64,2304]{2,1,0:T(8,128)(2,1)S(1)} %pad_maximum_fusion.5.own), channel_id=1, source_target_pairs={{0,4},{2,6},{4,0},{6,2},{8,12},{10,14},{12,8},{14,10},{16,20},{18,... | collective-permute-start | bytes 3538952 | tf_op jit(solution)/shard_map/ppermute | solution.py:20
  109.1 40.7 %collective-permute-start.26 = (bf16[4,64,2304]{2,1,0:T(8,128)(2,1)S(1)}, bf16[4,64,2304]{2,1,0:T(8,128)(2,1)S(1)}, u32[]{:S(2)}, u32[]{:S(2)}) collective-permute-start(bf16[4,64,2304]{2,1,0:T(8,128)(2,1)S(1)} %pad_maximum_fusion.5.own), channel_id=1, source_target_pairs={{0,2},{2,0},{4,6},{6,4},{8,10},{10,8},{12,14},{14,12},{16,18},{18,... | collective-permute-start | bytes 3538952 | tf_op jit(solution)/shard_map/ppermute | solution.py:20
  121.3 50.3 %collective-permute-start.20 = (bf16[4,64,2304]{2,1,0:T(8,128)(2,1)S(1)}, bf16[4,64,2304]{2,1,0:T(8,128)(2,1)S(1)}, u32[]{:S(2)}, u32[]{:S(2)}) collective-permute-start(bf16[4,64,2304]{2,1,0:T(8,128)(2,1)S(1)} %pad_maximum_fusion.4.own), channel_id=1, source_target_pairs={{0,4},{2,6},{4,0},{6,2},{8,12},{10,14},{12,8},{14,10},{16,20},{18,... | collective-permute-start | bytes 3538952 | tf_op jit(solution)/shard_map/ppermute | solution.py:20
  121.9 50.6 %collective-permute-start.19 = (bf16[4,64,2304]{2,1,0:T(8,128)(2,1)S(1)}, bf16[4,64,2304]{2,1,0:T(8,128)(2,1)S(1)}, u32[]{:S(2)}, u32[]{:S(2)}) collective-permute-start(bf16[4,64,2304]{2,1,0:T(8,128)(2,1)S(1)} %pad_maximum_fusion.4.own), channel_id=1, source_target_pairs={{0,2},{2,0},{4,6},{6,4},{8,10},{10,8},{12,14},{14,12},{16,18},{18,... | collective-permute-start | bytes 3538952 | tf_op jit(solution)/shard_map/ppermute | solution.py:20
  136.1 39.9 %collective-permute-start.14 = (bf16[2,64,2304]{2,1,0:T(8,128)(2,1)S(1)}, bf16[2,64,2304]{2,1,0:T(8,128)(2,1)S(1)}, u32[]{:S(2)}, u32[]{:S(2)}) collective-permute-start(bf16[2,64,2304]{2,1,0:T(8,128)(2,1)S(1)} %slice.317), channel_id=1, source_target_pairs={{0,2},{2,0},{4,6},{6,4},{8,10},{10,8},{12,14},{14,12},{16,18},{18,... | collective-permute-start | bytes 1769480 | tf_op jit(solution)/shard_map/ppermute | solution.py:20
  146.6 35.9 %collective-permute-start.15 = (bf16[2,64,2304]{2,1,0:T(8,128)(2,1)S(1)}, bf16[2,64,2304]{2,1,0:T(8,128)(2,1)S(1)}, u32[]{:S(2)}, u32[]{:S(2)}) collective-permute-start(bf16[2,64,2304]{2,1,0:T(8,128)(2,1)S(1)} %slice.318), channel_id=1, source_target_pairs={{0,4},{2,6},{4,0},{6,2},{8,12},{10,14},{12,8},{14,10},{16,20},{18,... | collective-permute-start | bytes 1769480 | tf_op jit(solution)/shard_map/ppermute | solution.py:20
  149.8 57.8 %collective-permute-start.8 = (bf16[1024,1024]{0,1:T(8,128)(2,1)}, bf16[1024,1024]{0,1:T(8,128)(2,1)}, u32[]{:S(2)}, u32[]{:S(2)}) collective-permute-start(bf16[1024,1024]{0,1:T(8,128)(2,1)} %convolution_convert_fusion.5), channel_id=1, source_target_pairs={{0,1},{1,0},{2,3},{3,2},{4,5},{5,4},{6,7},{7,6},{8,9},{9,8},{10,11... | collective-permute-start | bytes 6291464 | tf_op jit(solution)/shard_map/ppermute | solution.py:25
  287.8 129.8 %collective-permute-start.30 = (bf16[1024,1024]{0,1:T(8,128)(2,1)}, bf16[1024,1024]{0,1:T(8,128)(2,1)S(1)}, u32[]{:S(2)}, u32[]{:S(2)}) collective-permute-start(bf16[1024,1024]{0,1:T(8,128)(2,1)} %convolution_convert_fusion.4), channel_id=1, source_target_pairs={{0,1},{1,0},{2,3},{3,2},{4,5},{5,4},{6,7},{7,6},{8,9},{9,8},{10,11... | collective-permute-start | bytes 6291464 | tf_op jit(solution)/shard_map/ppermute | solution.py:25
  294.7 38.4 %collective-permute-start.60 = (bf16[4,64,2304]{2,1,0:T(8,128)(2,1)S(1)}, bf16[4,64,2304]{2,1,0:T(8,128)(2,1)S(1)}, u32[]{:S(2)}, u32[]{:S(2)}) collective-permute-start(bf16[4,64,2304]{2,1,0:T(8,128)(2,1)S(1)} %pad_maximum_fusion.10), channel_id=1, source_target_pairs={{0,4},{2,6},{4,0},{6,2},{8,12},{10,14},{12,8},{14,10},{16,20},{18,... | collective-permute-start | bytes 3538952 | tf_op jit(solution)/shard_map/ppermute | solution.py:20
  296.5 38.1 %collective-permute-start.62 = (bf16[4,64,2304]{2,1,0:T(8,128)(2,1)S(1)}, bf16[4,64,2304]{2,1,0:T(8,128)(2,1)S(1)}, u32[]{:S(2)}, u32[]{:S(2)}) collective-permute-start(bf16[4,64,2304]{2,1,0:T(8,128)(2,1)S(1)} %pad_maximum_fusion.11), channel_id=1, source_target_pairs={{0,2},{2,0},{4,6},{6,4},{8,10},{10,8},{12,14},{14,12},{16,18},{18,... | collective-permute-start | bytes 3538952 | tf_op jit(solution)/shard_map/ppermute | solution.py:20
  307.4 51.1 %collective-permute-start.53 = (bf16[4,64,2304]{2,1,0:T(8,128)(2,1)S(1)}, bf16[4,64,2304]{2,1,0:T(8,128)(2,1)S(1)}, u32[]{:S(2)}, u32[]{:S(2)}) collective-permute-start(bf16[4,64,2304]{2,1,0:T(8,128)(2,1)S(1)} %pad_maximum_fusion.8), channel_id=1, source_target_pairs={{0,4},{2,6},{4,0},{6,2},{8,12},{10,14},{12,8},{14,10},{16,20},{18,... | collective-permute-start | bytes 3538952 | tf_op jit(solution)/shard_map/ppermute | solution.py:20
  309.2 49.2 %collective-permute-start.55 = (bf16[4,64,2304]{2,1,0:T(8,128)(2,1)S(1)}, bf16[4,64,2304]{2,1,0:T(8,128)(2,1)S(1)}, u32[]{:S(2)}, u32[]{:S(2)}) collective-permute-start(bf16[4,64,2304]{2,1,0:T(8,128)(2,1)S(1)} %pad_maximum_fusion.9), channel_id=1, source_target_pairs={{0,2},{2,0},{4,6},{6,4},{8,10},{10,8},{12,14},{14,12},{16,18},{18,... | collective-permute-start | bytes 3538952 | tf_op jit(solution)/shard_map/ppermute | solution.py:20
  333.1 45.7 %collective-permute-start.46 = (bf16[4,64,2304]{2,1,0:T(8,128)(2,1)S(1)}, bf16[4,64,2304]{2,1,0:T(8,128)(2,1)S(1)}, u32[]{:S(2)}, u32[]{:S(2)}) collective-permute-start(bf16[4,64,2304]{2,1,0:T(8,128)(2,1)S(1)} %pad_maximum_fusion.6), channel_id=1, source_target_pairs={{0,4},{2,6},{4,0},{6,2},{8,12},{10,14},{12,8},{14,10},{16,20},{18,... | collective-permute-start | bytes 3538952 | tf_op jit(solution)/shard_map/ppermute | solution.py:20
  334.6 56.1 %collective-permute-start.48 = (bf16[4,64,2304]{2,1,0:T(8,128)(2,1)S(1)}, bf16[4,64,2304]{2,1,0:T(8,128)(2,1)S(1)}, u32[]{:S(2)}, u32[]{:S(2)}) collective-permute-start(bf16[4,64,2304]{2,1,0:T(8,128)(2,1)S(1)} %pad_maximum_fusion.7), channel_id=1, source_target_pairs={{0,2},{2,0},{4,6},{6,4},{8,10},{10,8},{12,14},{14,12},{16,18},{18,... | collective-permute-start | bytes 3538952 | tf_op jit(solution)/shard_map/ppermute | solution.py:20
  358.4 57.6 %collective-permute-start.31 = (bf16[1024,1024]{0,1:T(8,128)(2,1)S(1)}, bf16[1024,1024]{0,1:T(8,128)(2,1)S(1)}, u32[]{:S(2)}, u32[]{:S(2)}) collective-permute-start(bf16[1024,1024]{0,1:T(8,128)(2,1)S(1)} %add_convert_fusion), channel_id=1, source_target_pairs={{0,1},{1,0},{2,3},{3,2},{4,5},{5,4},{6,7},{7,6},{8,9},{9,8},{10,11... | collective-permute-start | bytes 6291464 | tf_op jit(solution)/shard_map/ppermute | solution.py:25
  358.4 36.7 %collective-permute-start.63 = (bf16[64,2304]{1,0:T(8,128)(2,1)S(1)}, bf16[64,2304]{1,0:T(8,128)(2,1)S(1)}, u32[]{:S(2)}, u32[]{:S(2)}) collective-permute-start(bf16[64,2304]{1,0:T(8,128)(2,1)S(1)} %get-tuple-element.70), channel_id=1, source_target_pairs={{0,8},{2,10},{4,12},{6,14},{8,0},{10,2},{12,4},{14,6},{16,24},{18,... | collective-permute-start | bytes 884744 | tf_op jit(solution)/shard_map/ppermute | solution.py:20
  378.8 34.4 %collective-permute-start.64 = (bf16[64,2304]{1,0:T(8,128)(2,1)S(1)}, bf16[64,2304]{1,0:T(8,128)(2,1)S(1)}, u32[]{:S(2)}, u32[]{:S(2)}) collective-permute-start(bf16[64,2304]{1,0:T(8,128)(2,1)S(1)} %get-tuple-element.72), channel_id=1, source_target_pairs={{0,16},{2,18},{4,20},{6,22},{8,24},{10,26},{12,28},{14,30},{16,0},... | collective-permute-start | bytes 884744 | tf_op jit(solution)/shard_map/ppermute | solution.py:20
  395.1 75.6 %collective-permute-start.56 = (bf16[64,2304]{1,0:T(8,128)(2,1)}, bf16[64,2304]{1,0:T(8,128)(2,1)S(1)}, u32[]{:S(2)}, u32[]{:S(2)}) collective-permute-start(bf16[64,2304]{1,0:T(8,128)(2,1)} %get-tuple-element.73), channel_id=1, source_target_pairs={{0,8},{2,10},{4,12},{6,14},{8,0},{10,2},{12,4},{14,6},{16,24},{18,... | collective-permute-start | bytes 884744 | tf_op jit(solution)/shard_map/ppermute | solution.py:20
  413.3 59.1 %collective-permute-start.57 = (bf16[64,2304]{1,0:T(8,128)(2,1)}, bf16[64,2304]{1,0:T(8,128)(2,1)}, u32[]{:S(2)}, u32[]{:S(2)}) collective-permute-start(bf16[64,2304]{1,0:T(8,128)(2,1)} %get-tuple-element.75), channel_id=1, source_target_pairs={{0,16},{2,18},{4,20},{6,22},{8,24},{10,26},{12,28},{14,30},{16,0},... | collective-permute-start | bytes 884744 | tf_op jit(solution)/shard_map/ppermute | solution.py:20
  413.3 59.1 %collective-permute-start.58 = (bf16[64,2304]{1,0:T(8,128)(2,1)}, bf16[64,2304]{1,0:T(8,128)(2,1)}, u32[]{:S(2)}, u32[]{:S(2)}) collective-permute-start(bf16[64,2304]{1,0:T(8,128)(2,1)} %get-tuple-element.74), channel_id=1, source_target_pairs={{0,24},{2,26},{4,28},{6,30},{8,16},{10,18},{12,20},{14,22},{16,8},... | collective-permute-start | bytes 884744 | tf_op jit(solution)/shard_map/ppermute | solution.py:20
  472.4 34.5 %collective-permute-start.33 = (bf16[1024,1024]{0,1:T(8,128)(2,1)}, bf16[1024,1024]{0,1:T(8,128)(2,1)}, u32[]{:S(2)}, u32[]{:S(2)}) collective-permute-start(bf16[1024,1024]{0,1:T(8,128)(2,1)} %fusion.28), channel_id=1, source_target_pairs={{0,1},{1,0},{2,3},{3,2},{4,5},{5,4},{6,7},{7,6},{8,9},{9,8},{10,11... | collective-permute-start | bytes 6291464 | tf_op jit(solution)/shard_map/ppermute | solution.py:25
  (113 other events, 1979.2 us)
